TPU v7x, 256 devices: a whole 4x4x8 slice. The times are simulated.
256 devices in a mesh: row: 32 (over y, x, core), col: 8 (over z).
Axes of the slice: x: 4, y: 4, z: 8, core: 2. Of those that a mesh axis runs over, the one named last changes fastest.
Arguments:
- features: bfloat16 [32768, 512], P(('row', 'col')), may hold values from -6 to 6
- tile_data: bfloat16 [256, 32, 2, 128, 128], P('row', 'col'), as said below
- tile_ids: int32 [256, 32, 2], P('row', 'col'), may hold values from 0 to 7, as said below
- tile_counts: int32 [256, 32], P('row', 'col'), may hold values from 0 to 2, as said below
- hist_tiles: bfloat16 [256, 8, 128, 128], P('row', 'col'), may hold values from -0.1875 to 0.1875
- hist_ids: int32 [256, 8], P('row', 'col'), may hold values from 0 to 31
- hist_cache: bfloat16 [4096, 512], P('col'), may hold values from -6 to 6
- first_weight: bfloat16 [512, 512], replicated, may hold values from -0.25 to 0.25
- second_weight: bfloat16 [512, 512], replicated, may hold values from -0.25 to 0.25
- grad_out: bfloat16 [32768, 512], P(('row', 'col')), may hold values from -6 to 6
Outputs:
- embedding: bfloat16 [32768, 512], P(('row', 'col'))
- grad_first: float32 [512, 512], replicated
- grad_second: float32 [512, 512], replicated
Inputs may be any that keep to these rules, and one draw needn't show every extreme that they name: tile_ids[p, j, t] is a tile column within panel j; slots t >= tile_counts[p, j] are padding and must be ignored; the used slots of a tile row and panel name distinct columns; the matrix that the tiles describe is symmetric. `tile_counts`: the count depends only on the block row of the tile row and on the panel. `tile_data`: padded slots hold arbitrary values.
All inputs are finite; a program needn't handle non-finite values.
Results may differ from a plain program's by a relative error of at most 0.018.
Values may be sent and summed in bfloat16 or wider, within the bound.
No kernel may reach another device: no remote copies, remote signals or barrier semaphores. Data moves between devices by JAX's collectives and lax.ppermute only.
A program may use at most 128 MiB of HBM per device.

v0:
```python
import math
import jax
import jax.numpy as jnp
from jax import lax
from jax.sharding import PartitionSpec as P


def spread(shard, axis, root):
    mine = lax.axis_index(axis) == root
    return lax.psum(jnp.where(mine, shard, jnp.zeros_like(shard)), axis)


def pick_tiles(panel_rows, tile_data, tile_ids, tile_counts):
    tile_rows = tile_ids.shape[0]
    slot_count = tile_ids.shape[1]
    tile_size = tile_data.shape[-1]
    blocks = panel_rows.reshape(tile_rows, tile_size, panel_rows.shape[1])
    picked = blocks[tile_ids]
    keep_mask = (jnp.arange(slot_count)[None, :] < tile_counts[:, None]).astype(tile_data.dtype)
    masked = tile_data * keep_mask[:, :, None, None]
    product = jnp.einsum("atij,atjf->aif", masked, picked, preferred_element_type=jnp.float32)
    return product.reshape(tile_rows * tile_size, panel_rows.shape[1])


def aggregate(source, tile_data, tile_ids, tile_counts):
    section_total = tile_data.shape[1]
    col_index = lax.axis_index("col")
    running = jnp.zeros(source.shape, jnp.float32)
    for section_num in range(section_total):
        panel_rows = spread(source, "row", col_index * section_total + section_num)
        running = running + pick_tiles(
            panel_rows,
            tile_data[:, section_num],
            tile_ids[:, section_num],
            tile_counts[:, section_num],
        )
    return running


def local(
    features,
    tile_data,
    tile_ids,
    tile_counts,
    hist_tiles,
    hist_ids,
    hist_cache,
    first_weight,
    second_weight,
    grad_out,
):
    share_rows = features.shape[0]
    node_count = share_rows * lax.axis_size("row") * lax.axis_size("col")
    norm_scale = 1.0 / math.sqrt(node_count)
    contract_rows = (((0,), (0,)), ((), ()))
    feat_panel = lax.all_gather(features, "col", axis=0, tiled=True)
    first_sum = aggregate(feat_panel, tile_data, tile_ids, tile_counts)
    first_agg = lax.psum_scatter(
        first_sum.astype(jnp.bfloat16), "col", scatter_dimension=0, tiled=True
    )
    first_pre = jnp.dot(first_agg, first_weight, preferred_element_type=jnp.float32)
    hidden_share = jax.nn.silu(first_pre).astype(jnp.bfloat16)
    hidden_panel = lax.all_gather(hidden_share, "col", axis=0, tiled=True)
    second_sum = aggregate(hidden_panel, tile_data, tile_ids, tile_counts)
    tile_size = hist_tiles.shape[-1]
    feat_width = hist_cache.shape[1]
    whole_cache = lax.all_gather(hist_cache, "col", axis=0, tiled=True)
    cache_blocks = whole_cache.reshape(-1, tile_size, feat_width)
    picked = cache_blocks[hist_ids]
    history = jnp.einsum("ahij,ahjf->aif", hist_tiles, picked, preferred_element_type=jnp.float32)
    second_sum = second_sum + history.reshape(second_sum.shape)
    second_agg = lax.psum_scatter(
        second_sum.astype(jnp.bfloat16), "col", scatter_dimension=0, tiled=True
    )
    embedding = jnp.dot(second_agg, second_weight, preferred_element_type=jnp.float32).astype(
        jnp.bfloat16
    )
    grad_agg = lax.dot_general(
        grad_out, second_weight, (((1,), (1,)), ((), ())), preferred_element_type=jnp.float32
    ).astype(jnp.bfloat16)
    second_term = (
        lax.dot_general(second_agg, grad_out, contract_rows, preferred_element_type=jnp.float32)
        * norm_scale
    )
    grad_second = lax.psum(second_term, ("row", "col"))
    grad_panel = lax.all_gather(grad_agg, "col", axis=0, tiled=True)
    back_sum = aggregate(grad_panel, tile_data, tile_ids, tile_counts)
    grad_hidden = lax.psum_scatter(
        back_sum.astype(jnp.bfloat16), "col", scatter_dimension=0, tiled=True
    )
    sigmoid_gate = jax.nn.sigmoid(first_pre)
    grad_pre = (
        grad_hidden.astype(jnp.float32) * sigmoid_gate * (1.0 + first_pre * (1.0 - sigmoid_gate))
    ).astype(jnp.bfloat16)
    first_term = (
        lax.dot_general(first_agg, grad_pre, contract_rows, preferred_element_type=jnp.float32)
        * norm_scale
    )
    grad_first = lax.psum(first_term, ("row", "col"))
    return (embedding, grad_first, grad_second)


def solution(mesh):
    placed = (
        P(("row", "col"), None),
        P("row", "col", None, None, None),
        P("row", "col", None),
        P("row", "col"),
        P("row", "col", None, None),
        P("row", "col"),
        P("col", None),
        P(),
        P(),
        P(("row", "col"), None),
    )
    return jax.shard_map(
        local,
        mesh=mesh,
        in_specs=placed,
        out_specs=(P(("row", "col"), None), P(), P()),
        check_vma=False,
    )
```

profile of v0, /device:TPU:2, one launch (start us, length us, event | category | flops | bytes accessed | tf_op | source)
XLA Modules:
  0.0 899.5 jit_solution(7173406365842705599)
XLA Ops:
  10.2 41.6 %all-gather.11.cloned.1.call-done = bf16[1024,512]{1,0:T(8,128)(2,1)} async-done(((bf16[128,512]{1,0:T(8,128)(2,1)}), bf16[1024,512]{1,0:T(8,128)(2,1)}) %all-gather.11.cloned.1.call-update) | async-done | bytes 1048592 | tf_op jit(solution)/shard_map/all_gather | solution.py:86
  51.8 38.6 %all-gather.5.cloned.1.call-done = bf16[1024,512]{1,0:T(8,128)(2,1)} async-done(((bf16[128,512]{1,0:T(8,128)(2,1)}), bf16[1024,512]{1,0:T(8,128)(2,1)}) %all-gather.5.cloned.1.call-update) | async-done | bytes 1048592 | tf_op jit(solution)/shard_map/all_gather | solution.py:56
  90.4 4.9 broadcast_select_fusion
  97.0 118.1 %all-reduce.11.cloned.1.call-done = (bf16[8,128,512]{2,1,0:T(8,128)(2,1)}, bf16[8,128,512]{2,1,0:T(8,128)(2,1)}, bf16[8,128,512]{2,1,0:T(8,128)(2,1)}, bf16[8,128,512]{2,1,0:T(8,128)(2,1)}) async-done(((bf16[8,128,512]{2,1,0:T(8,128)(2,1)}, bf16[8,128,512]{2,1,0:T(8,128)(2,1)}, bf16[8,128,512]{2,1,0:T(8,128)(2,1)}, bf16[8,128,512]{2,1,0:T(8,128)(2,1)}), (bf16[8,128,512]{2,1,0:T(8,128)(2,1)}, ...) | async-done | bytes 4194320 | tf_op jit(solution)/shard_map/psum | solution.py:10
  218.3 3.4 gather_fusion.1
  221.8 3.6 fusion.5
  227.2 3.3 gather_fusion.2
  230.5 3.5 fusion.11
  237.3 5.1 fusion.2
  242.4 39.5 %reduce-scatter.4.cloned.1.call-done = bf16[128,512]{1,0:T(8,128)(2,1)} async-done(((bf16[1024,512]{1,0:T(8,128)(2,1)}), bf16[128,512]{1,0:T(8,128)(2,1)}) %reduce-scatter.4.cloned.1.call-update) | async-done | bytes 131088 | tf_op jit(solution)/shard_map/reduce_scatter | solution.py:58
  284.4 36.8 %all-gather.7.cloned.1.call-done = bf16[1024,512]{1,0:T(8,128)(2,1)} async-done(((bf16[128,512]{1,0:T(8,128)(2,1)}), bf16[1024,512]{1,0:T(8,128)(2,1)}) %all-gather.7.cloned.1.call-update) | async-done | bytes 1048592 | tf_op jit(solution)/shard_map/all_gather | solution.py:63
  321.2 3.3 broadcast_select_fusion.10
  325.2 50.8 %all-gather.9.cloned.1.call-done = bf16[4096,512]{1,0:T(8,128)(2,1)} async-done(((bf16[512,512]{1,0:T(8,128)(2,1)}), bf16[4096,512]{1,0:T(8,128)(2,1)}) %all-gather.9.cloned.1.call-update) | async-done | bytes 4194320 | tf_op jit(solution)/shard_map/all_gather | solution.py:67
  376.0 3.8 gather_fusion.8
  379.8 130.5 %all-reduce.9.cloned.1.call-done = (bf16[8,128,512]{2,1,0:T(8,128)(2,1)}, bf16[8,128,512]{2,1,0:T(8,128)(2,1)}, bf16[8,128,512]{2,1,0:T(8,128)(2,1)}, bf16[8,128...) async-done(((bf16[8,128,512]{2,1,0:T(8,128)(2,1)}, ...) | async-done | bytes 8388624 | tf_op jit(solution)/shard_map/psum | solution.py:10
  513.5 3.4 fusion.4
  520.2 3.4 fusion.7
  523.6 3.3 gather_fusion.6
  527.0 3.5 fusion.10
  530.4 3.3 gather_fusion.7
  536.6 3.6 fusion.1
  560.6 19.0 %reduce-scatter.6.cloned.1.call-done = bf16[128,512]{1,0:T(8,128)(2,1)} async-done(((bf16[1024,512]{1,0:T(8,128)(2,1)}), bf16[128,512]{1,0:T(8,128)(2,1)}) %reduce-scatter.6.cloned.1.call-update) | async-done | bytes 131088 | tf_op jit(solution)/shard_map/reduce_scatter | solution.py:72
  581.8 38.6 %reduce-scatter.8.cloned.1.call-done = bf16[128,512]{1,0:T(8,128)(2,1)} async-done(((bf16[1024,512]{1,0:T(8,128)(2,1)}), bf16[128,512]{1,0:T(8,128)(2,1)}) %reduce-scatter.8.cloned.1.call-update) | async-done | bytes 131088 | tf_op jit(solution)/shard_map/reduce_scatter | solution.py:88
  623.5 265.8 %all-reduce.7.cloned.1.call-done = (f32[512,512]{1,0:T(8,128)}, f32[512,512]{1,0:T(8,128)}) async-done(((f32[512,512]{1,0:T(8,128)}, f32[512,512]{1,0:T(8,128)}), (f32[512,512]{1,0:T(8,128)}, f32[512,512]{1,0:T(8,128)})) %all-reduce.7.cloned.1.call-update) | async-done | bytes 2097168 | tf_op jit(solution)/shard_map/psum | solution.py:99
  (96 shorter events, 54.5 us)
Async XLA Ops:
  7.2 274.7 %copy-start = (bf16[512,512]{1,0:T(8,128)(2,1)S(1)}, bf16[512,512]{1,0:T(8,128)(2,1)}, u32[]{:S(2)}) copy-start(bf16[512,512]{1,0:T(8,128)(2,1)} %param.17) | copy-start | bytes 1572868
  7.2 44.6 %all-gather.11.cloned.1.call-start = ((), (), s32[]{:S(2)}) async-start(), calls=%async_computation.8 | async-start | bytes 1179648 | tf_op jit(solution)/shard_map/all_gather | solution.py:86
  9.4 81.0 %all-gather.5.cloned.1.call-start = ((), (), s32[]{:S(2)}) async-start(), calls=%async_computation.3 | async-start | bytes 1179648 | tf_op jit(solution)/shard_map/all_gather | solution.py:56
  10.1 205.0 %all-reduce.11.cloned.1.call-start = ((), (), s32[]{:S(2)}) async-start(), calls=%async_computation.12 | async-start | bytes 8388608 | tf_op jit(solution)/shard_map/psum | solution.py:10
  95.3 186.6 %reduce-scatter.4.cloned.1.call-start = ((), (), s32[]{:S(2)}) async-start(), calls=%async_computation.4 | async-start | bytes 1179648 | tf_op jit(solution)/shard_map/reduce_scatter | solution.py:58
  218.3 3.4 copy-start.2
  221.8 3.6 copy-start.5
  242.4 78.8 %all-gather.7.cloned.1.call-start = ((), (), s32[]{:S(2)}) async-start(), calls=%async_computation.5 | async-start | bytes 1179648 | tf_op jit(solution)/shard_map/all_gather | solution.py:63
  283.8 92.3 %all-gather.9.cloned.1.call-start = ((), (), s32[]{:S(2)}) async-start(), calls=%async_computation.6 | async-start | bytes 4718592 | tf_op jit(solution)/shard_map/all_gather | solution.py:67
  284.3 225.9 %all-reduce.9.cloned.1.call-start = ((), (), s32[]{:S(2)}) async-start(), calls=%async_computation.11 | async-start | bytes 16777216 | tf_op jit(solution)/shard_map/psum | solution.py:10
  324.6 255.0 %reduce-scatter.6.cloned.1.call-start = ((), (), s32[]{:S(2)}) async-start(), calls=%async_computation.7 | async-start | bytes 1179648 | tf_op jit(solution)/shard_map/reduce_scatter | solution.py:72
  533.7 2.2 copy-start.7
  533.7 2.9 copy-start.8
  533.7 2.9 copy-start.13
  540.2 80.1 %reduce-scatter.8.cloned.1.call-start = ((), (), s32[]{:S(2)}) async-start(), calls=%async_computation.9 | async-start | bytes 1179648 | tf_op jit(solution)/shard_map/reduce_scatter | solution.py:88
  553.4 2.2 copy-start.3
  557.2 1.6 copy-start.6
  558.8 20.7 %copy-start.11 = (bf16[128,512]{1,0:T(8,128)(2,1)S(1)}, bf16[128,512]{1,0:T(8,128)(2,1)}, u32[]{:S(2)}) copy-start(bf16[128,512]{1,0:T(8,128)(2,1)} %param.19) | copy-start | bytes 393220
  560.5 59.8 %copy-start.16 = (bf16[128,512]{1,0:T(8,128)(2,1)S(1)}, bf16[128,512]{1,0:T(8,128)(2,1)}, u32[]{:S(2)}) copy-start(bf16[128,512]{1,0:T(8,128)(2,1)} %reduce-scatter.4.cloned.1.call-done) | copy-start | bytes 393220
  560.5 328.8 %all-reduce.7.cloned.1.call-start = ((), (), s32[]{:S(2)}) async-start(), calls=%async_computation.10 | async-start | bytes 4194304 | tf_op jit(solution)/shard_map/psum | solution.py:99
  581.8 40.8 %copy-start.9 = (bf16[512,512]{1,0:T(8,128)(2,1)S(1)}, bf16[512,512]{1,0:T(8,128)(2,1)}, u32[]{:S(2)}) copy-start(bf16[512,512]{1,0:T(8,128)(2,1)} %param.18) | copy-start | bytes 1572868
  581.8 40.9 %copy-start.12 = (bf16[128,512]{1,0:T(8,128)(2,1)S(1)}, bf16[128,512]{1,0:T(8,128)(2,1)}, u32[]{:S(2)}) copy-start(bf16[128,512]{1,0:T(8,128)(2,1)} %reduce-scatter.6.cloned.1.call-done) | copy-start | bytes 393220
  889.3 2.4 copy-start.10
  889.3 3.4 copy-start.1
  (4 other events, 4.3 us)
Sparse Core Ops, SparseCore 0:
  10.3 41.3 all-gather.10
  53.5 36.7 all-gather.4
  95.5 119.5 all-reduce.10
  242.5 39.3 reduce-scatter.3
  284.1 37.0 all-gather.6
  322.9 53.1 all-gather.8
  380.7 129.5 all-reduce.8
  540.4 39.1 reduce-scatter.5
  582.7 37.6 reduce-scatter.7
  626.3 262.9 all-reduce.6
where the time goes:
time: 901 us; the launch traced here: 900 us
  waiting for transfers between devices  781 us (87%)
  local copies, waits for them, and re-layouts  51.3 us (6%)
  matrix products  44.3 us (5%)
  between operations  14.3 us (2%)
    psum x1, waiting for transfers between devices, local(): grad_first = lax.psum(first_term, ('row', 'col'))  266 us
    psum x2, waiting for transfers between devices, spread(): return lax.psum(jnp.where(mine, shard, jnp.zeros_like(shard)), axis)  249 us
    all_gather x1, waiting for transfers between devices, local(): whole_cache = lax.all_gather(hist_cache, 'col', axis=0, tiled=True)  50.8 us
    all_gather x1, waiting for transfers between devices, local(): grad_panel = lax.all_gather(grad_agg, 'col', axis=0, tiled=True)  41.6 us
    gather x12, local copies, waits for them, and re-layouts, pick_tiles(): picked = blocks[tile_ids]  39.5 us
    reduce_scatter x1, waiting for transfers between devices, local(): lax.psum_scatter(first_sum.astype(jnp.bfloat16), 'col', scatter_dimension...  39.5 us
    all_gather x1, waiting for transfers between devices, local(): feat_panel = lax.all_gather(features, 'col', axis=0, tiled=True)  38.6 us
    reduce_scatter x1, waiting for transfers between devices, local(): lax.psum_scatter(back_sum.astype(jnp.bfloat16), 'col', scatter_dimension=...  38.6 us
  transfers between devices with their start and end apart: 10, of which 10 were waited for; matrix products, arithmetic and copies ran while one was open for 3% of the time, Pallas kernels for 0%

commit v1 on v0

--- a/solution.py
+++ b/solution.py
@@ -3,6 +3,24 @@
 import jax.numpy as jnp
 from jax import lax
 from jax.sharding import PartitionSpec as P
+
+
+def collect(array, axis, dim):
+    ways, here, hop = (lax.axis_size(axis), lax.axis_index(axis), array.shape[dim])
+    shape = [n * ways if d == dim else n for d, n in enumerate(array.shape)]
+    full = lax.dynamic_update_slice_in_dim(
+        jnp.zeros(shape, array.dtype), array, here * hop, axis=dim
+    )
+    going_up = going_down = array
+    for far in range(1, ways // 2 + 1):
+        going_up = lax.ppermute(going_up, axis, [(d, (d + 1) % ways) for d in range(ways)])
+        full = lax.dynamic_update_slice_in_dim(full, going_up, (here - far) % ways * hop, axis=dim)
+        if 2 * far < ways:
+            going_down = lax.ppermute(going_down, axis, [(d, (d - 1) % ways) for d in range(ways)])
+            full = lax.dynamic_update_slice_in_dim(
+                full, going_down, (here + far) % ways * hop, axis=dim
+            )
+    return full
 
 
 def spread(shard, axis, root):
@@ -83,7 +101,7 @@
         * norm_scale
     )
     grad_second = lax.psum(second_term, ("row", "col"))
-    grad_panel = lax.all_gather(grad_agg, "col", axis=0, tiled=True)
+    grad_panel = collect(grad_agg, "col", 0)
     back_sum = aggregate(grad_panel, tile_data, tile_ids, tile_counts)
     grad_hidden = lax.psum_scatter(
         back_sum.astype(jnp.bfloat16), "col", scatter_dimension=0, tiled=True

time: 901 us -> 861 us (0.956)
  waiting for transfers between devices: 781 us -> 730 us
  starting transfers between devices: 0.41 us -> 13.5 us
    all_gather x1 -> x0, waiting for transfers between devices: 41.6 us -> none  [local(): grad_panel = lax.all_gather(grad_agg, 'col', axis=0, tiled=True)]
    all_gather x1, waiting for transfers between devices: 38.6 us -> 12.3 us  [local(): feat_panel = lax.all_gather(features, 'col', axis=0, tiled=True)]
    ppermute x0 -> x7, waiting for transfers between devices: none -> 16.5 us  [the longest x4 14.4 us: collect(): lax.ppermute(going_up, axis, [(d, (d + 1) % ways) for d in range(ways)])]
    ppermute x0 -> x7, starting transfers between devices: none -> 13 us  [the longest x3 10.9 us: collect(): lax.ppermute(going_down, axis, [(d, (d - 1) % ways) for d in range(ways)])]
  transfers between devices with their start and end apart: 10 -> 16, of which waited for: 10 -> 15; matrix products, arithmetic and copies ran while one was open for 3% -> 4% of each run, Pallas kernels for 0% -> 0%
where the time goes in v1:
time: 861 us; the launch traced here: 860 us
  waiting for transfers between devices  730 us (85%)
  local copies, waits for them, and re-layouts  51.3 us (6%)
  matrix products  43.5 us (5%)
  between operations  14 us (2%)
  starting transfers between devices  13.5 us (2%)
    psum x1, waiting for transfers between devices, local(): grad_first = lax.psum(first_term, ('row', 'col'))  266 us
    psum x2, waiting for transfers between devices, spread(): return lax.psum(jnp.where(mine, shard, jnp.zeros_like(shard)), axis)  249 us
    all_gather x1, waiting for transfers between devices, local(): whole_cache = lax.all_gather(hist_cache, 'col', axis=0, tiled=True)  50.8 us
    reduce_scatter x1, waiting for transfers between devices, local(): lax.psum_scatter(first_sum.astype(jnp.bfloat16), 'col', scatter_dimension...  39.5 us
    gather x12, local copies, waits for them, and re-layouts, pick_tiles(): picked = blocks[tile_ids]  39.4 us
    reduce_scatter x1, waiting for transfers between devices, local(): lax.psum_scatter(back_sum.astype(jnp.bfloat16), 'col', scatter_dimension=...  38.5 us
    all_gather x1, waiting for transfers between devices, local(): hidden_panel = lax.all_gather(hidden_share, 'col', axis=0, tiled=True)  36.8 us
    dot_general x12, matrix products, pick_tiles(): jnp.einsum('atij,atjf->aif', masked, picked, preferred_element_type=jnp.f...  31.4 us
  transfers between devices with their start and end apart: 16, of which 15 were waited for; matrix products, arithmetic and copies ran while one was open for 4% of the time, Pallas kernels for 0%

profile of v1, /device:TPU:2, one launch (start us, length us, event | category | flops | bytes accessed | tf_op | source)
XLA Modules:
  0.0 860.1 jit_solution(14592207221688713583)
XLA Ops:
  11.4 4.0 collective-permute-start.1
  15.5 3.4 collective-permute-done
  25.9 3.7 collective-permute-start.5
  32.8 6.2 collective-permute-done.6
  39.0 12.3 %all-gather.4.cloned.1.call-done = bf16[1024,512]{1,0:T(8,128)(2,1)} async-done(((bf16[128,512]{1,0:T(8,128)(2,1)}), bf16[1024,512]{1,0:T(8,128)(2,1)}) %all-gather.4.cloned.1.call-update) | async-done | bytes 1048592 | tf_op jit(solution)/shard_map/all_gather | solution.py:74
  51.3 4.6 broadcast_select_fusion
  57.6 118.6 %all-reduce.11.cloned.1.call-done = (bf16[8,128,512]{2,1,0:T(8,128)(2,1)}, bf16[8,128,512]{2,1,0:T(8,128)(2,1)}, bf16[8,128,512]{2,1,0:T(8,128)(2,1)}, bf16[8,128,512]{2,1,0:T(8,128)(2,1)}) async-done(((bf16[8,128,512]{2,1,0:T(8,128)(2,1)}, bf16[8,128,512]{2,1,0:T(8,128)(2,1)}, bf16[8,128,512]{2,1,0:T(8,128)(2,1)}, bf16[8,128,512]{2,1,0:T(8,128)(2,1)}), (bf16[8,128,512]{2,1,0:T(8,128)(2,1)}, ...) | async-done | bytes 4194320 | tf_op jit(solution)/shard_map/psum | solution.py:28
  179.4 3.4 gather_fusion.1
  182.9 3.6 fusion.5
  191.6 3.4 fusion.11
  198.3 5.1 fusion.2
  203.5 39.5 %reduce-scatter.4.cloned.1.call-done = bf16[128,512]{1,0:T(8,128)(2,1)} async-done(((bf16[1024,512]{1,0:T(8,128)(2,1)}), bf16[128,512]{1,0:T(8,128)(2,1)}) %reduce-scatter.4.cloned.1.call-update) | async-done | bytes 131088 | tf_op jit(solution)/shard_map/reduce_scatter | solution.py:76
  245.5 36.8 %all-gather.6.cloned.1.call-done = bf16[1024,512]{1,0:T(8,128)(2,1)} async-done(((bf16[128,512]{1,0:T(8,128)(2,1)}), bf16[1024,512]{1,0:T(8,128)(2,1)}) %all-gather.6.cloned.1.call-update) | async-done | bytes 1048592 | tf_op jit(solution)/shard_map/all_gather | solution.py:81
  282.3 3.3 broadcast_select_fusion.10
  286.3 50.8 %all-gather.8.cloned.1.call-done = bf16[4096,512]{1,0:T(8,128)(2,1)} async-done(((bf16[512,512]{1,0:T(8,128)(2,1)}), bf16[4096,512]{1,0:T(8,128)(2,1)}) %all-gather.8.cloned.1.call-update) | async-done | bytes 4194320 | tf_op jit(solution)/shard_map/all_gather | solution.py:85
  337.1 3.8 gather_fusion.8
  340.9 130.3 %all-reduce.9.cloned.1.call-done = (bf16[8,128,512]{2,1,0:T(8,128)(2,1)}, bf16[8,128,512]{2,1,0:T(8,128)(2,1)}, bf16[8,128,512]{2,1,0:T(8,128)(2,1)}, bf16[8,128...) async-done(((bf16[8,128,512]{2,1,0:T(8,128)(2,1)}, ...) | async-done | bytes 8388624 | tf_op jit(solution)/shard_map/psum | solution.py:28
  474.4 3.4 fusion.4
  481.1 3.4 fusion.7
  487.8 3.4 fusion.10
  497.4 3.6 fusion.1
  521.4 19.0 %reduce-scatter.6.cloned.1.call-done = bf16[128,512]{1,0:T(8,128)(2,1)} async-done(((bf16[1024,512]{1,0:T(8,128)(2,1)}), bf16[128,512]{1,0:T(8,128)(2,1)}) %reduce-scatter.6.cloned.1.call-update) | async-done | bytes 131088 | tf_op jit(solution)/shard_map/reduce_scatter | solution.py:90
  542.6 38.5 %reduce-scatter.8.cloned.1.call-done = bf16[128,512]{1,0:T(8,128)(2,1)} async-done(((bf16[1024,512]{1,0:T(8,128)(2,1)}), bf16[128,512]{1,0:T(8,128)(2,1)}) %reduce-scatter.8.cloned.1.call-update) | async-done | bytes 131088 | tf_op jit(solution)/shard_map/reduce_scatter | solution.py:106
  584.3 265.9 %all-reduce.7.cloned.1.call-done = (f32[512,512]{1,0:T(8,128)}, f32[512,512]{1,0:T(8,128)}) async-done(((f32[512,512]{1,0:T(8,128)}, f32[512,512]{1,0:T(8,128)}), (f32[512,512]{1,0:T(8,128)}, f32[512,512]{1,0:T(8,128)})) %all-reduce.7.cloned.1.call-update) | async-done | bytes 2097168 | tf_op jit(solution)/shard_map/psum | solution.py:117
  (113 shorter events, 75.8 us)
Async XLA Ops:
  7.2 44.1 %all-gather.4.cloned.1.call-start = ((), (), s32[]{:S(2)}) async-start(), calls=%async_computation.3 | async-start | bytes 1179648 | tf_op jit(solution)/shard_map/all_gather | solution.py:74
  7.9 168.3 %all-reduce.11.cloned.1.call-start = ((), (), s32[]{:S(2)}) async-start(), calls=%async_computation.11 | async-start | bytes 8388608 | tf_op jit(solution)/shard_map/psum | solution.py:28
  9.4 9.4 %collective-permute-start = (bf16[128,512]{1,0:T(8,128)(2,1)S(1)}, bf16[128,512]{1,0:T(8,128)(2,1)S(1)}, u32[]{:S(2)}, u32[]{:S(2)}) collective-permute-start(bf16[128,512]{1,0:T(8,128)(2,1)S(1)} %get-tuple-element.40), channel_id=1, source_target_pairs={{0,1},{1,2},{2,3},{3,4},{4,5},{5,6},{6,7},{7,0},{8,9},{9,10},{10,1... | collective-permute-start | bytes 393224 | tf_op jit(solution)/shard_map/ppermute | solution.py:16
  11.4 7.4 collective-permute-start.1
  18.9 6.2 collective-permute-start.2
  18.9 7.1 collective-permute-start.3
  25.0 6.5 collective-permute-start.4
  25.9 6.9 collective-permute-start.5
  31.6 7.5 collective-permute-start.6
  55.9 187.1 %reduce-scatter.4.cloned.1.call-start = ((), (), s32[]{:S(2)}) async-start(), calls=%async_computation.4 | async-start | bytes 1179648 | tf_op jit(solution)/shard_map/reduce_scatter | solution.py:76
  179.4 3.4 copy-start.1
  182.9 3.6 copy-start.4
  198.3 44.7 %copy-start.14 = (bf16[512,512]{1,0:T(8,128)(2,1)S(1)}, bf16[512,512]{1,0:T(8,128)(2,1)}, u32[]{:S(2)}) copy-start(bf16[512,512]{1,0:T(8,128)(2,1)} %param.17) | copy-start | bytes 1572868
  203.5 78.8 %all-gather.6.cloned.1.call-start = ((), (), s32[]{:S(2)}) async-start(), calls=%async_computation.5 | async-start | bytes 1179648 | tf_op jit(solution)/shard_map/all_gather | solution.py:81
  244.9 92.2 %all-gather.8.cloned.1.call-start = ((), (), s32[]{:S(2)}) async-start(), calls=%async_computation.6 | async-start | bytes 4718592 | tf_op jit(solution)/shard_map/all_gather | solution.py:85
  245.5 225.7 %all-reduce.9.cloned.1.call-start = ((), (), s32[]{:S(2)}) async-start(), calls=%async_computation.10 | async-start | bytes 16777216 | tf_op jit(solution)/shard_map/psum | solution.py:28
  285.6 254.7 %reduce-scatter.6.cloned.1.call-start = ((), (), s32[]{:S(2)}) async-start(), calls=%async_computation.7 | async-start | bytes 1179648 | tf_op jit(solution)/shard_map/reduce_scatter | solution.py:90
  494.6 2.9 copy-start.7
  494.6 2.9 copy-start.11
  501.1 80.0 %reduce-scatter.8.cloned.1.call-start = ((), (), s32[]{:S(2)}) async-start(), calls=%async_computation.8 | async-start | bytes 1179648 | tf_op jit(solution)/shard_map/reduce_scatter | solution.py:106
  519.6 20.7 %copy-start.9 = (bf16[128,512]{1,0:T(8,128)(2,1)S(1)}, bf16[128,512]{1,0:T(8,128)(2,1)}, u32[]{:S(2)}) copy-start(bf16[128,512]{1,0:T(8,128)(2,1)} %param.19) | copy-start | bytes 393220
  521.3 59.8 %copy-start.15 = (bf16[128,512]{1,0:T(8,128)(2,1)S(1)}, bf16[128,512]{1,0:T(8,128)(2,1)}, u32[]{:S(2)}) copy-start(bf16[128,512]{1,0:T(8,128)(2,1)} %reduce-scatter.4.cloned.1.call-done) | copy-start | bytes 393220
  521.3 328.9 %all-reduce.7.cloned.1.call-start = ((), (), s32[]{:S(2)}) async-start(), calls=%async_computation.9 | async-start | bytes 4194304 | tf_op jit(solution)/shard_map/psum | solution.py:117
  542.6 40.8 %copy-start.10 = (bf16[128,512]{1,0:T(8,128)(2,1)S(1)}, bf16[128,512]{1,0:T(8,128)(2,1)}, u32[]{:S(2)}) copy-start(bf16[128,512]{1,0:T(8,128)(2,1)} %reduce-scatter.6.cloned.1.call-done) | copy-start | bytes 393220
  (9 other events, 13.8 us)
Sparse Core Ops, SparseCore 0:
  9.8 41.4 all-gather.3
  56.1 120.0 all-reduce.10
  203.6 39.3 reduce-scatter.3
  245.2 37.0 all-gather.5
  283.9 53.1 all-gather.7
  341.7 129.5 all-reduce.8
  501.2 39.1 reduce-scatter.5
  543.5 37.6 reduce-scatter.7
  587.3 262.9 all-reduce.6
